TPU v7x, 128 devices: a whole 4x4x4 slice. The times are simulated.
128 devices in a mesh: blk: 16 (over z_hi, x, core), head: 8 (over y, z_lo).
Axes of the slice: x: 4, y: 4, z: 4 (z_hi: 2, z_lo: 2; z = z_hi * 2 + z_lo), core: 2. Of those that a mesh axis runs over, the one named last changes fastest.
Arguments:
- queries: bfloat16 [8192, 8192], P('blk', 'head'), may hold values from -120 to 120
- keys: bfloat16 [8192, 1024], P('blk', 'head'), may hold values from -6.5 to 6.5
- values: bfloat16 [8192, 1024], P('blk', 'head'), may hold values from -6 to 6
- w_out: bfloat16 [8192, 8192], P('head'), may hold values from -0.09375 to 0.09375
- order: int32 [32], replicated, may hold values from 0 to 31, each once
Outputs:
- mixed: bfloat16 [8192, 8192], P('blk', 'head')
Inputs may be any that keep to these rules, and one draw needn't show every extreme that they name: `order`: A permutation of 0 to 31.
All inputs are finite; a program needn't handle non-finite values.
Results may differ from a plain program's by a relative error of at most 0.015.
Values may be sent and summed in bfloat16 or wider, within the bound.
A program may use at most 128 MiB of HBM per device.

v0:
```python
import math

import jax
import jax.numpy as jnp
from jax import lax
from jax.sharding import Mesh
from jax.sharding import PartitionSpec as P

HD = 128
HEAD = ("head_0", "head_1")


def sent_together(arrays, axis, dim, along):
    both = jnp.concatenate(arrays, axis=along)
    filled, at, finished = (lax.all_gather(both, axis, axis=dim, tiled=True), 0, [])
    for a in arrays:
        finished.append(lax.slice_in_dim(filled, at, at + a.shape[along], axis=along))
        at += a.shape[along]
    return tuple(finished)


def sum_by_axis(value, axes, dim):
    for axis in axes:
        value = lax.psum_scatter(value, axis, scatter_dimension=dim, tiled=True)
    return value


def positions(order, rows, half):
    count = order.shape[0]
    block_id = rows // half
    hit = block_id[:, None] == jnp.arange(count, dtype=jnp.int32)[None, :]
    return jnp.sum(jnp.where(hit, order[None, :], 0), axis=1) * half + rows % half


def attend(carry, k_block, v_block, key_pos, q_heads, query_pos, scale):
    top, total, summed = carry
    score = (
        jnp.einsum("kgtd,nkd->kgtn", q_heads, k_block, preferred_element_type=jnp.float32) * scale
    )
    visible = key_pos[None, None, None, :] <= query_pos[None, None, :, None]
    score = jnp.where(visible, score, -1e30)
    new_top = jnp.maximum(top, jnp.max(score, axis=-1))
    weight = jnp.where(visible, jnp.exp(score - new_top[..., None]), 0.0)
    factor = jnp.exp(top - new_top)
    total = total * factor + jnp.sum(weight, axis=-1)
    summed = summed * factor[..., None] + jnp.einsum(
        "kgtn,nkd->kgtd", weight.astype(jnp.bfloat16), v_block, preferred_element_type=jnp.float32
    )
    return (new_top, total, summed)


def per_device(queries, keys, values, w_out, order):
    tok = queries.shape[0]
    half = tok // 2
    head_size = HD
    kv_local = keys.shape[1] // head_size
    q_local = queries.shape[1] // head_size
    group = q_local // kv_local
    scale = head_size ** (-0.5)
    own = lax.axis_index("blk") * tok + jnp.arange(tok, dtype=jnp.int32)
    query_pos = positions(order, own, half)
    q_heads = jnp.transpose(queries.reshape(tok, kv_local, group, head_size), (1, 2, 0, 3))
    start_state = (
        jnp.full((kv_local, group, tok), -1e30, jnp.float32),
        jnp.zeros((kv_local, group, tok), jnp.float32),
        jnp.zeros((kv_local, group, tok, head_size), jnp.float32),
    )
    every = sent_together((keys, values), "blk", 0, 1)
    k_piece, v_piece = every
    count = k_piece.shape[0]
    width = math.gcd(count, 512)
    steps = count // width
    k_blocks = k_piece.reshape(steps, width, kv_local, head_size)
    v_blocks = v_piece.reshape(steps, width, kv_local, head_size)

    def one_block(state, inputs):
        k_block, v_block, number = inputs
        rows = 0 + number * width + jnp.arange(width, dtype=jnp.int32)
        key_pos = positions(order, rows, half)
        return (attend(state, k_block, v_block, key_pos, q_heads, query_pos, scale), None)

    result, _ = lax.scan(
        one_block, start_state, (k_blocks, v_blocks, jnp.arange(steps, dtype=jnp.int32))
    )
    top, total, summed = result
    attended = (summed / total[..., None]).astype(jnp.bfloat16)
    attended = jnp.transpose(attended, (2, 0, 1, 3)).reshape(tok, q_local * head_size)
    partial_out = jnp.dot(attended, w_out, preferred_element_type=jnp.float32)
    return (
        sum_by_axis(partial_out.astype(jnp.bfloat16), HEAD, 1)
        .astype(jnp.float32)
        .astype(jnp.bfloat16)
    )


def solution(mesh):
    finer = Mesh(mesh.devices.reshape(mesh.shape["blk"], 4, 2), ("blk", "head_0", "head_1"))
    placed = (P("blk", HEAD), P("blk", HEAD), P("blk", HEAD), P(HEAD, None), P())
    return jax.shard_map(
        per_device, mesh=finer, in_specs=placed, out_specs=P("blk", HEAD), check_vma=False
    )
```

profile of v0, /device:TPU:0, one launch (start us, length us, event | category | flops | bytes accessed | tf_op | source)
XLA Modules:
  0.0 477.5 jit_solution(11019423978983539975)
XLA Ops:
  6.5 1.7 pad_maximum_fusion
  8.4 1.5 copy.12
  9.9 0.7 copy.13
  10.6 0.7 select_reduce_fusion.1
  11.3 57.2 %all-gather.2.cloned.1.call-done = bf16[8192,256]{1,0:T(8,128)(2,1)} async-done(((bf16[512,256]{1,0:T(8,128)(2,1)}), bf16[8192,256]{1,0:T(8,128)(2,1)}) %all-gather.2.cloned.1.call-update) | async-done | bytes 4194320 | tf_op jit(solution)/shard_map/all_gather | solution.py:15
  68.5 3.9 fusion.28
  72.4 263.5 %while.17 = (s32[]{:T(128)}, f32[1,8,512]{2,1,0:T(8,128)S(1)}, f32[1,8,512]{2,1,0:T(8,128)S(1)}, f32[1,8,512,128]{3,2,1,0:T(8,128)}, s32[16]{0:T(128)S(1)}, /*in...) while((s32[]{:T(128)}, f32[1,8,512]{2,1,0:T(8,128)S(1)}, ...), condition=%wide.region_5.6_spmd.clone, body=%wide.region_1.5_spmd.clone.sunk | while | flops 1102928384 | bytes 65551176 | solution.py:82
  74.0 4.7 fusion.40
  78.7 7.5 %bitcast_add_fusion.5 = f32[1,8,512,128]{3,2,1,0:T(8,128)} fusion(f32[1,8,512,128]{3,2,1,0:T(8,128)} %get-tuple-element.300, f32[512,8,512]{2,0,1:T(8,128)} %get-tuple-element.282, f32[8,512]{1,0:T(8,128)S(1)} %bitcast.74, pred[512,512]{0,1:T(8,128)(4,1)S(1)} %broadcast_compare_fusion.2, f32[8,512]{1,0:T(8,128)S(1)} %get-tuple-element.283, ...), kind=kOutput, calls=%fused_computation.7.clone.1 | convolution fusion | flops 548929536 | bytes 13009409 | tf_op jit(solution)/shard_map/while/body/eval_jaxpr/kgtn,nkd->kgtd/dot_general | solution.py:46
  86.2 2.0 fusion.42
  88.2 0.6 dynamic_slice.38
  89.8 4.7 fusion.40
  94.6 8.1 %bitcast_add_fusion.5 = f32[1,8,512,128]{3,2,1,0:T(8,128)} fusion(f32[1,8,512,128]{3,2,1,0:T(8,128)} %get-tuple-element.300, f32[512,8,512]{2,0,1:T(8,128)} %get-tuple-element.282, f32[8,512]{1,0:T(8,128)S(1)} %bitcast.74, pred[512,512]{0,1:T(8,128)(4,1)S(1)} %broadcast_compare_fusion.2, f32[8,512]{1,0:T(8,128)S(1)} %get-tuple-element.283, ...), kind=kOutput, calls=%fused_computation.7.clone.1 | convolution fusion | flops 548929536 | bytes 13009409 | tf_op jit(solution)/shard_map/while/body/eval_jaxpr/kgtn,nkd->kgtd/dot_general | solution.py:46
  102.7 2.0 fusion.42
  104.8 0.6 dynamic_slice.38
  106.3 4.7 fusion.40
  111.1 8.1 %bitcast_add_fusion.5 = f32[1,8,512,128]{3,2,1,0:T(8,128)} fusion(f32[1,8,512,128]{3,2,1,0:T(8,128)} %get-tuple-element.300, f32[512,8,512]{2,0,1:T(8,128)} %get-tuple-element.282, f32[8,512]{1,0:T(8,128)S(1)} %bitcast.74, pred[512,512]{0,1:T(8,128)(4,1)S(1)} %broadcast_compare_fusion.2, f32[8,512]{1,0:T(8,128)S(1)} %get-tuple-element.283, ...), kind=kOutput, calls=%fused_computation.7.clone.1 | convolution fusion | flops 548929536 | bytes 13009409 | tf_op jit(solution)/shard_map/while/body/eval_jaxpr/kgtn,nkd->kgtd/dot_general | solution.py:46
  119.2 2.0 fusion.42
  121.3 0.6 dynamic_slice.38
  122.9 4.7 fusion.40
  127.6 8.1 %bitcast_add_fusion.5 = f32[1,8,512,128]{3,2,1,0:T(8,128)} fusion(f32[1,8,512,128]{3,2,1,0:T(8,128)} %get-tuple-element.300, f32[512,8,512]{2,0,1:T(8,128)} %get-tuple-element.282, f32[8,512]{1,0:T(8,128)S(1)} %bitcast.74, pred[512,512]{0,1:T(8,128)(4,1)S(1)} %broadcast_compare_fusion.2, f32[8,512]{1,0:T(8,128)S(1)} %get-tuple-element.283, ...), kind=kOutput, calls=%fused_computation.7.clone.1 | convolution fusion | flops 548929536 | bytes 13009409 | tf_op jit(solution)/shard_map/while/body/eval_jaxpr/kgtn,nkd->kgtd/dot_general | solution.py:46
  135.7 2.0 fusion.42
  137.8 0.6 dynamic_slice.38
  139.4 4.7 fusion.40
  144.1 8.1 %bitcast_add_fusion.5 = f32[1,8,512,128]{3,2,1,0:T(8,128)} fusion(f32[1,8,512,128]{3,2,1,0:T(8,128)} %get-tuple-element.300, f32[512,8,512]{2,0,1:T(8,128)} %get-tuple-element.282, f32[8,512]{1,0:T(8,128)S(1)} %bitcast.74, pred[512,512]{0,1:T(8,128)(4,1)S(1)} %broadcast_compare_fusion.2, f32[8,512]{1,0:T(8,128)S(1)} %get-tuple-element.283, ...), kind=kOutput, calls=%fused_computation.7.clone.1 | convolution fusion | flops 548929536 | bytes 13009409 | tf_op jit(solution)/shard_map/while/body/eval_jaxpr/kgtn,nkd->kgtd/dot_general | solution.py:46
  152.2 2.0 fusion.42
  154.3 0.6 dynamic_slice.38
  155.9 4.7 fusion.40
  160.6 8.1 %bitcast_add_fusion.5 = f32[1,8,512,128]{3,2,1,0:T(8,128)} fusion(f32[1,8,512,128]{3,2,1,0:T(8,128)} %get-tuple-element.300, f32[512,8,512]{2,0,1:T(8,128)} %get-tuple-element.282, f32[8,512]{1,0:T(8,128)S(1)} %bitcast.74, pred[512,512]{0,1:T(8,128)(4,1)S(1)} %broadcast_compare_fusion.2, f32[8,512]{1,0:T(8,128)S(1)} %get-tuple-element.283, ...), kind=kOutput, calls=%fused_computation.7.clone.1 | convolution fusion | flops 548929536 | bytes 13009409 | tf_op jit(solution)/shard_map/while/body/eval_jaxpr/kgtn,nkd->kgtd/dot_general | solution.py:46
  168.7 2.0 fusion.42
  172.4 4.7 fusion.40
  177.1 8.1 %bitcast_add_fusion.5 = f32[1,8,512,128]{3,2,1,0:T(8,128)} fusion(f32[1,8,512,128]{3,2,1,0:T(8,128)} %get-tuple-element.300, f32[512,8,512]{2,0,1:T(8,128)} %get-tuple-element.282, f32[8,512]{1,0:T(8,128)S(1)} %bitcast.74, pred[512,512]{0,1:T(8,128)(4,1)S(1)} %broadcast_compare_fusion.2, f32[8,512]{1,0:T(8,128)S(1)} %get-tuple-element.283, ...), kind=kOutput, calls=%fused_computation.7.clone.1 | convolution fusion | flops 548929536 | bytes 13009409 | tf_op jit(solution)/shard_map/while/body/eval_jaxpr/kgtn,nkd->kgtd/dot_general | solution.py:46
  185.2 2.0 fusion.42
  188.9 4.7 fusion.40
  193.6 8.1 %bitcast_add_fusion.5 = f32[1,8,512,128]{3,2,1,0:T(8,128)} fusion(f32[1,8,512,128]{3,2,1,0:T(8,128)} %get-tuple-element.300, f32[512,8,512]{2,0,1:T(8,128)} %get-tuple-element.282, f32[8,512]{1,0:T(8,128)S(1)} %bitcast.74, pred[512,512]{0,1:T(8,128)(4,1)S(1)} %broadcast_compare_fusion.2, f32[8,512]{1,0:T(8,128)S(1)} %get-tuple-element.283, ...), kind=kOutput, calls=%fused_computation.7.clone.1 | convolution fusion | flops 548929536 | bytes 13009409 | tf_op jit(solution)/shard_map/while/body/eval_jaxpr/kgtn,nkd->kgtd/dot_general | solution.py:46
  201.8 2.0 fusion.42
  205.4 4.7 fusion.40
  210.1 8.1 %bitcast_add_fusion.5 = f32[1,8,512,128]{3,2,1,0:T(8,128)} fusion(f32[1,8,512,128]{3,2,1,0:T(8,128)} %get-tuple-element.300, f32[512,8,512]{2,0,1:T(8,128)} %get-tuple-element.282, f32[8,512]{1,0:T(8,128)S(1)} %bitcast.74, pred[512,512]{0,1:T(8,128)(4,1)S(1)} %broadcast_compare_fusion.2, f32[8,512]{1,0:T(8,128)S(1)} %get-tuple-element.283, ...), kind=kOutput, calls=%fused_computation.7.clone.1 | convolution fusion | flops 548929536 | bytes 13009409 | tf_op jit(solution)/shard_map/while/body/eval_jaxpr/kgtn,nkd->kgtd/dot_general | solution.py:46
  218.3 2.0 fusion.42
  221.9 4.7 fusion.40
  226.6 8.1 %bitcast_add_fusion.5 = f32[1,8,512,128]{3,2,1,0:T(8,128)} fusion(f32[1,8,512,128]{3,2,1,0:T(8,128)} %get-tuple-element.300, f32[512,8,512]{2,0,1:T(8,128)} %get-tuple-element.282, f32[8,512]{1,0:T(8,128)S(1)} %bitcast.74, pred[512,512]{0,1:T(8,128)(4,1)S(1)} %broadcast_compare_fusion.2, f32[8,512]{1,0:T(8,128)S(1)} %get-tuple-element.283, ...), kind=kOutput, calls=%fused_computation.7.clone.1 | convolution fusion | flops 548929536 | bytes 13009409 | tf_op jit(solution)/shard_map/while/body/eval_jaxpr/kgtn,nkd->kgtd/dot_general | solution.py:46
  234.8 2.0 fusion.42
  238.4 4.7 fusion.40
  243.2 8.1 %bitcast_add_fusion.5 = f32[1,8,512,128]{3,2,1,0:T(8,128)} fusion(f32[1,8,512,128]{3,2,1,0:T(8,128)} %get-tuple-element.300, f32[512,8,512]{2,0,1:T(8,128)} %get-tuple-element.282, f32[8,512]{1,0:T(8,128)S(1)} %bitcast.74, pred[512,512]{0,1:T(8,128)(4,1)S(1)} %broadcast_compare_fusion.2, f32[8,512]{1,0:T(8,128)S(1)} %get-tuple-element.283, ...), kind=kOutput, calls=%fused_computation.7.clone.1 | convolution fusion | flops 548929536 | bytes 13009409 | tf_op jit(solution)/shard_map/while/body/eval_jaxpr/kgtn,nkd->kgtd/dot_general | solution.py:46
  251.3 2.0 fusion.42
  254.9 4.7 fusion.40
  259.7 8.1 %bitcast_add_fusion.5 = f32[1,8,512,128]{3,2,1,0:T(8,128)} fusion(f32[1,8,512,128]{3,2,1,0:T(8,128)} %get-tuple-element.300, f32[512,8,512]{2,0,1:T(8,128)} %get-tuple-element.282, f32[8,512]{1,0:T(8,128)S(1)} %bitcast.74, pred[512,512]{0,1:T(8,128)(4,1)S(1)} %broadcast_compare_fusion.2, f32[8,512]{1,0:T(8,128)S(1)} %get-tuple-element.283, ...), kind=kOutput, calls=%fused_computation.7.clone.1 | convolution fusion | flops 548929536 | bytes 13009409 | tf_op jit(solution)/shard_map/while/body/eval_jaxpr/kgtn,nkd->kgtd/dot_general | solution.py:46
  267.8 2.0 fusion.42
  271.5 4.7 fusion.40
  276.2 8.1 %bitcast_add_fusion.5 = f32[1,8,512,128]{3,2,1,0:T(8,128)} fusion(f32[1,8,512,128]{3,2,1,0:T(8,128)} %get-tuple-element.300, f32[512,8,512]{2,0,1:T(8,128)} %get-tuple-element.282, f32[8,512]{1,0:T(8,128)S(1)} %bitcast.74, pred[512,512]{0,1:T(8,128)(4,1)S(1)} %broadcast_compare_fusion.2, f32[8,512]{1,0:T(8,128)S(1)} %get-tuple-element.283, ...), kind=kOutput, calls=%fused_computation.7.clone.1 | convolution fusion | flops 548929536 | bytes 13009409 | tf_op jit(solution)/shard_map/while/body/eval_jaxpr/kgtn,nkd->kgtd/dot_general | solution.py:46
  284.3 2.0 fusion.42
  288.0 4.7 fusion.40
  292.7 8.1 %bitcast_add_fusion.5 = f32[1,8,512,128]{3,2,1,0:T(8,128)} fusion(f32[1,8,512,128]{3,2,1,0:T(8,128)} %get-tuple-element.300, f32[512,8,512]{2,0,1:T(8,128)} %get-tuple-element.282, f32[8,512]{1,0:T(8,128)S(1)} %bitcast.74, pred[512,512]{0,1:T(8,128)(4,1)S(1)} %broadcast_compare_fusion.2, f32[8,512]{1,0:T(8,128)S(1)} %get-tuple-element.283, ...), kind=kOutput, calls=%fused_computation.7.clone.1 | convolution fusion | flops 548929536 | bytes 13009409 | tf_op jit(solution)/shard_map/while/body/eval_jaxpr/kgtn,nkd->kgtd/dot_general | solution.py:46
  300.8 2.0 fusion.42
  304.5 4.7 fusion.40
  309.2 8.1 %bitcast_add_fusion.5 = f32[1,8,512,128]{3,2,1,0:T(8,128)} fusion(f32[1,8,512,128]{3,2,1,0:T(8,128)} %get-tuple-element.300, f32[512,8,512]{2,0,1:T(8,128)} %get-tuple-element.282, f32[8,512]{1,0:T(8,128)S(1)} %bitcast.74, pred[512,512]{0,1:T(8,128)(4,1)S(1)} %broadcast_compare_fusion.2, f32[8,512]{1,0:T(8,128)S(1)} %get-tuple-element.283, ...), kind=kOutput, calls=%fused_computation.7.clone.1 | convolution fusion | flops 548929536 | bytes 13009409 | tf_op jit(solution)/shard_map/while/body/eval_jaxpr/kgtn,nkd->kgtd/dot_general | solution.py:46
  317.3 2.0 fusion.42
  321.0 4.7 fusion.40
  325.7 8.1 %bitcast_add_fusion.5 = f32[1,8,512,128]{3,2,1,0:T(8,128)} fusion(f32[1,8,512,128]{3,2,1,0:T(8,128)} %get-tuple-element.300, f32[512,8,512]{2,0,1:T(8,128)} %get-tuple-element.282, f32[8,512]{1,0:T(8,128)S(1)} %bitcast.74, pred[512,512]{0,1:T(8,128)(4,1)S(1)} %broadcast_compare_fusion.2, f32[8,512]{1,0:T(8,128)S(1)} %get-tuple-element.283, ...), kind=kOutput, calls=%fused_computation.7.clone.1 | convolution fusion | flops 548929536 | bytes 13009409 | tf_op jit(solution)/shard_map/while/body/eval_jaxpr/kgtn,nkd->kgtd/dot_general | solution.py:46
  333.8 2.0 fusion.42
  335.9 1.9 copy.14
  338.1 17.0 %convolution_convert_fusion = bf16[512,8192]{1,0:T(8,128)(2,1)} fusion(bf16[512,1024]{0,1:T(8,128)(2,1)S(1)} %bitcast.79, bf16[1024,8192]{1,0:T(8,128)(2,1)} %param.10), kind=kOutput, calls=%fused_computation.39 | convolution fusion | flops 8594128896 | bytes 26214400 | tf_op jit(solution)/shard_map/dot_general | solution.py:88
  355.2 79.2 %reduce-scatter.3.cloned.1.call-done = bf16[512,2048]{1,0:T(8,128)(2,1)} async-done(((bf16[512,8192]{1,0:T(8,128)(2,1)}), bf16[512,2048]{1,0:T(8,128)(2,1)}) %reduce-scatter.3.cloned.1.call-update) | async-done | bytes 2097168 | tf_op jit(solution)/shard_map/reduce_scatter | solution.py:24
  434.4 36.6 %reduce-scatter.5.cloned.1.call-done = bf16[512,1024]{1,0:T(8,128)(2,1)} async-done(((bf16[512,2048]{1,0:T(8,128)(2,1)}), bf16[512,1024]{1,0:T(8,128)(2,1)}) %reduce-scatter.5.cloned.1.call-update) | async-done | bytes 1048592 | tf_op jit(solution)/shard_map/reduce_scatter | solution.py:24
  (170 shorter events, 12.7 us)
Async XLA Ops:
  6.5 65.8 %copy-start.1 = (s32[32]{0:T(128)S(1)}, s32[32]{0:T(128)}, u32[]{:S(2)}) copy-start(s32[32]{0:T(128)} %param.11) | copy-start | bytes 388
  6.5 61.9 %all-gather.2.cloned.1.call-start = ((), (), s32[]{:S(2)}) async-start(), calls=%async_computation.2 | async-start | bytes 4456448 | tf_op jit(solution)/shard_map/all_gather | solution.py:15
  8.3 426.1 %reduce-scatter.3.cloned.1.call-start = ((), (), s32[]{:S(2)}) async-start(), calls=%async_computation.3 | async-start | bytes 10485760 | tf_op jit(solution)/shard_map/reduce_scatter | solution.py:24
  78.7 7.5 %copy-start = (f32[512,8,512]{2,0,1:T(8,128)S(1)}, f32[512,8,512]{2,0,1:T(8,128)}, u32[]{:S(2)}) copy-start(f32[512,8,512]{2,0,1:T(8,128)} %get-tuple-element.282) | copy-start | bytes 25165828 | tf_op jit(solution)/shard_map/while
  94.5 8.1 %copy-start = (f32[512,8,512]{2,0,1:T(8,128)S(1)}, f32[512,8,512]{2,0,1:T(8,128)}, u32[]{:S(2)}) copy-start(f32[512,8,512]{2,0,1:T(8,128)} %get-tuple-element.282) | copy-start | bytes 25165828 | tf_op jit(solution)/shard_map/while
  111.1 8.1 %copy-start = (f32[512,8,512]{2,0,1:T(8,128)S(1)}, f32[512,8,512]{2,0,1:T(8,128)}, u32[]{:S(2)}) copy-start(f32[512,8,512]{2,0,1:T(8,128)} %get-tuple-element.282) | copy-start | bytes 25165828 | tf_op jit(solution)/shard_map/while
  127.6 8.1 %copy-start = (f32[512,8,512]{2,0,1:T(8,128)S(1)}, f32[512,8,512]{2,0,1:T(8,128)}, u32[]{:S(2)}) copy-start(f32[512,8,512]{2,0,1:T(8,128)} %get-tuple-element.282) | copy-start | bytes 25165828 | tf_op jit(solution)/shard_map/while
  144.1 8.1 %copy-start = (f32[512,8,512]{2,0,1:T(8,128)S(1)}, f32[512,8,512]{2,0,1:T(8,128)}, u32[]{:S(2)}) copy-start(f32[512,8,512]{2,0,1:T(8,128)} %get-tuple-element.282) | copy-start | bytes 25165828 | tf_op jit(solution)/shard_map/while
  160.6 8.1 %copy-start = (f32[512,8,512]{2,0,1:T(8,128)S(1)}, f32[512,8,512]{2,0,1:T(8,128)}, u32[]{:S(2)}) copy-start(f32[512,8,512]{2,0,1:T(8,128)} %get-tuple-element.282) | copy-start | bytes 25165828 | tf_op jit(solution)/shard_map/while
  177.1 8.1 %copy-start = (f32[512,8,512]{2,0,1:T(8,128)S(1)}, f32[512,8,512]{2,0,1:T(8,128)}, u32[]{:S(2)}) copy-start(f32[512,8,512]{2,0,1:T(8,128)} %get-tuple-element.282) | copy-start | bytes 25165828 | tf_op jit(solution)/shard_map/while
  193.6 8.1 %copy-start = (f32[512,8,512]{2,0,1:T(8,128)S(1)}, f32[512,8,512]{2,0,1:T(8,128)}, u32[]{:S(2)}) copy-start(f32[512,8,512]{2,0,1:T(8,128)} %get-tuple-element.282) | copy-start | bytes 25165828 | tf_op jit(solution)/shard_map/while
  210.1 8.1 %copy-start = (f32[512,8,512]{2,0,1:T(8,128)S(1)}, f32[512,8,512]{2,0,1:T(8,128)}, u32[]{:S(2)}) copy-start(f32[512,8,512]{2,0,1:T(8,128)} %get-tuple-element.282) | copy-start | bytes 25165828 | tf_op jit(solution)/shard_map/while
  226.6 8.1 %copy-start = (f32[512,8,512]{2,0,1:T(8,128)S(1)}, f32[512,8,512]{2,0,1:T(8,128)}, u32[]{:S(2)}) copy-start(f32[512,8,512]{2,0,1:T(8,128)} %get-tuple-element.282) | copy-start | bytes 25165828 | tf_op jit(solution)/shard_map/while
  243.1 8.1 %copy-start = (f32[512,8,512]{2,0,1:T(8,128)S(1)}, f32[512,8,512]{2,0,1:T(8,128)}, u32[]{:S(2)}) copy-start(f32[512,8,512]{2,0,1:T(8,128)} %get-tuple-element.282) | copy-start | bytes 25165828 | tf_op jit(solution)/shard_map/while
  259.7 8.1 %copy-start = (f32[512,8,512]{2,0,1:T(8,128)S(1)}, f32[512,8,512]{2,0,1:T(8,128)}, u32[]{:S(2)}) copy-start(f32[512,8,512]{2,0,1:T(8,128)} %get-tuple-element.282) | copy-start | bytes 25165828 | tf_op jit(solution)/shard_map/while
  276.2 8.1 %copy-start = (f32[512,8,512]{2,0,1:T(8,128)S(1)}, f32[512,8,512]{2,0,1:T(8,128)}, u32[]{:S(2)}) copy-start(f32[512,8,512]{2,0,1:T(8,128)} %get-tuple-element.282) | copy-start | bytes 25165828 | tf_op jit(solution)/shard_map/while
  292.7 8.1 %copy-start = (f32[512,8,512]{2,0,1:T(8,128)S(1)}, f32[512,8,512]{2,0,1:T(8,128)}, u32[]{:S(2)}) copy-start(f32[512,8,512]{2,0,1:T(8,128)} %get-tuple-element.282) | copy-start | bytes 25165828 | tf_op jit(solution)/shard_map/while
  309.2 8.1 %copy-start = (f32[512,8,512]{2,0,1:T(8,128)S(1)}, f32[512,8,512]{2,0,1:T(8,128)}, u32[]{:S(2)}) copy-start(f32[512,8,512]{2,0,1:T(8,128)} %get-tuple-element.282) | copy-start | bytes 25165828 | tf_op jit(solution)/shard_map/while
  325.7 8.1 %copy-start = (f32[512,8,512]{2,0,1:T(8,128)S(1)}, f32[512,8,512]{2,0,1:T(8,128)}, u32[]{:S(2)}) copy-start(f32[512,8,512]{2,0,1:T(8,128)} %get-tuple-element.282) | copy-start | bytes 25165828 | tf_op jit(solution)/shard_map/while
  355.1 115.9 %reduce-scatter.5.cloned.1.call-start = ((), (), s32[]{:S(2)}) async-start(), calls=%async_computation.4 | async-start | bytes 3145728 | tf_op jit(solution)/shard_map/reduce_scatter | solution.py:24
Sparse Core Ops, SparseCore 0:
  9.8 58.6 all-gather.1
  355.2 79.1 reduce-scatter.2
  436.8 34.1 reduce-scatter.4
where the time goes:
time: 478 us
  matrix products  222 us (46%)
  waiting for transfers between devices  173 us (36%)
  other arithmetic  40.7 us (9%)
  local copies, waits for them, and re-layouts  17.5 us (4%)
  between operations  13.2 us (3%)
  loops' own time  11.5 us (2%)
    dot_general x16, matrix products, attend(): jnp.einsum('kgtn,nkd->kgtd', weight.astype(jnp.bfloat16), v_block, prefer...  130 us
    reduce_scatter x2, waiting for transfers between devices, sum_by_axis(): value = lax.psum_scatter(value, axis, scatter_dimension=dim, tiled=True)  116 us
    dot_general x16, matrix products, attend(): jnp.einsum('kgtd,nkd->kgtn', q_heads, k_block, preferred_element_type=jnp...  75.1 us
    all_gather x1, waiting for transfers between devices, sent_together(): lax.all_gather(both, axis, axis=dim, tiled=True)  57.2 us
    reduce_sum x16, other arithmetic, attend(): total = total * factor + jnp.sum(weight, axis=-1)  32.2 us
    dot_general x1, matrix products, per_device(): partial_out = jnp.dot(attended, w_out, preferred_element_type=jnp.float32)  17 us
    another operation x1, loops' own time, per_device(): lax.scan(one_block, start_state, (k_blocks, v_blocks, jnp.arange(steps, d...  11.5 us
  transfers between devices with their start and end apart: 3, of which 3 were waited for; matrix products, arithmetic and copies ran while one was open for 1% of the time, Pallas kernels for 0%

commit v1 on v0

v1 whole, which is shorter than its diff:
```python
import jax
import jax.numpy as jnp
from jax import lax
from jax.experimental import pallas as pl
from jax.experimental.pallas import tpu as pltpu
from jax.sharding import PartitionSpec as P

HD = 128
CHUNK = 128
CHUNKS = 4
HEADS = 8
SUBS = 4
ZCOLS = 384
YCOLS = 640
SCALE2 = HD**-0.5 * 1.4426950408889634
HIDDEN = -1e30
MESH = pl.DeviceIdType.MESH
BF = jnp.bfloat16
F32 = jnp.float32
FAR, NEAR, ZSUM, ZPRE, ZFAR, ZNEAR = 0, 2, 6, 7, 8, 10


def mod(a, n):
    return lax.rem(a, n)


def div(a, n):
    return lax.div(a, n)


def kernel(
    order, q, k, v, w_hbm, out,
    kv, w, eye, masks, top, acc, att,
    py, pz, far, near, zsum, zpre, zfar, znear,
    kv_send, kv_recv, send, recv, w_sem,
):
    blk = lax.axis_index("blk")
    head = lax.axis_index("head")
    core = mod(blk, 2)
    x = mod(div(blk, 2), 4)
    zh = div(blk, 8)
    y = div(head, 2)
    zl = mod(head, 2)

    def block(dz, dx):
        return (mod(zh + dz, 2) * 4 + mod(x + dx, 4)) * 2 + core

    left, right, across = block(0, 3), block(0, 1), block(1, 0)
    mate = blk + 1 - 2 * core
    up = mod(y + 1, 4) * 2 + zl
    down = mod(y + 3, 4) * 2 + zl
    zmate = head + 1 - 2 * zl

    barrier = pltpu.get_barrier_semaphore()
    for peer in (left, right, across, mate):
        pl.semaphore_signal(barrier, inc=1, device_id=(peer, head), device_id_type=MESH)
    for peer in (up, down, zmate):
        pl.semaphore_signal(barrier, inc=1, device_id=(blk, peer), device_id_type=MESH)
    pl.semaphore_wait(barrier, 7)

    w_copy = pltpu.make_async_copy(w_hbm, w, w_sem)

    kv_sends = []

    def pass_on(source, part, to, own=False):
        ref = (k, v)[part] if own else kv.at[source, part]
        copy = pltpu.make_async_remote_copy(
            src_ref=ref, dst_ref=kv.at[source, part],
            send_sem=kv_send.at[len(kv_sends)], recv_sem=kv_recv.at[source, part],
            device_id=(to, head), device_id_type=MESH,
        )
        kv_sends.append(0)
        copy.start()

    def arrived(source, part):
        pltpu.make_async_remote_copy(
            src_ref=kv.at[source, part], dst_ref=kv.at[source, part],
            send_sem=kv_send.at[0], recv_sem=kv_recv.at[source, part],
            device_id=(mate, head), device_id_type=MESH,
        ).wait_recv()

    def mate_has(dz, dx):
        source = block(dz, dx) + 1 - 2 * core
        arrived(source, 0)
        arrived(source, 1)

    for to in (across, right, left, mate):
        for part in (0, 1):
            pass_on(blk, part, to, own=True)
    w_copy.start()

    kv[blk, 0] = k[...]
    kv[blk, 1] = v[...]
    row = lax.broadcasted_iota(jnp.int32, (128, 128), 0)
    col = lax.broadcasted_iota(jnp.int32, (128, 128), 1)
    eye[...] = jnp.where(row == col, 1.0, 0.0).astype(BF)
    masks[0] = jnp.zeros((128, 128), BF)
    masks[1] = jnp.where(row > col, HIDDEN, 0.0).astype(BF)
    masks[2] = jnp.full((128, 128), HIDDEN, BF)

    def gather_0():
        arrived(left, 0)
        pass_on(left, 0, right)
        arrived(right, 1)
        pass_on(right, 1, left)
        arrived(right, 0)
        arrived(left, 1)
        for part in (0, 1):
            pass_on(right, part, mate)
        for part in (0, 1):
            pass_on(left, part, mate)
        for part in (0, 1):
            arrived(across, part)
            pass_on(across, part, right)
            pass_on(across, part, left)
        for part in (0, 1):
            pass_on(across, part, mate)
        mate_has(0, 0)
        mate_has(0, 1)

    def gather_1():
        far_block = block(0, 2)
        for part in (0, 1):
            arrived(far_block, part)
            pass_on(far_block, part, mate)
        mate_has(0, 3)
        mate_has(1, 0)

    def gather_2():
        zleft, zright = block(1, 3), block(1, 1)
        arrived(zleft, 0)
        pass_on(zleft, 0, right)
        arrived(zright, 1)
        pass_on(zright, 1, left)
        arrived(zleft, 1)
        arrived(zright, 0)
        for source in (zleft, zright):
            for part in (0, 1):
                pass_on(source, part, mate)
        mate_has(0, 2)
        mate_has(1, 3)

    def gather_3():
        zfar_block = block(1, 2)
        for part in (0, 1):
            arrived(zfar_block, part)
            pass_on(zfar_block, part, mate)
        mate_has(1, 1)
        mate_has(1, 2)

    def attend(c, s):
        rows = pl.ds(pl.multiple_of(c * CHUNK, CHUNK), CHUNK)
        query_pos = 2 * order[2 * blk + div(c, 2)] + mod(c, 2)
        chips = (
            mod(zh + div(s, 3), 2) * 4 + mod(x + 4 - s, 4),
            mod(zh + div(s + 2, 3), 2) * 4 + mod(x + 5 - s, 4),
        )
        key_rows, value_rows = [], []
        ones = jnp.ones((128, 128), BF)
        for chip in chips:
            for b in (2 * chip, 2 * chip + 1):
                for t in range(4):
                    key_pos = 2 * order[2 * b + t // 2] + t % 2
                    kind = (key_pos > query_pos).astype(jnp.int32) + (
                        key_pos >= query_pos
                    ).astype(jnp.int32)
                    part = slice(t * 128, (t + 1) * 128)
                    key_rows.append(jnp.concatenate([kv[b, 0, part, :], masks[kind]], axis=1))
                    value_rows.append(jnp.concatenate([kv[b, 1, part, :], ones], axis=1))
        key_tile = jnp.concatenate(key_rows, axis=0)
        value_tile = jnp.concatenate(value_rows, axis=0)
        for u in range(SUBS):
            q_rows = [
                jnp.concatenate([q[rows, h * HD : (h + 1) * HD], eye[...]], axis=1)
                for h in (2 * u, 2 * u + 1)
            ]
            score = lax.dot_general(
                jnp.concatenate(q_rows, axis=0), key_tile,
                (((1,), (1,)), ((), ())), preferred_element_type=F32,
            )
            old = top[u]
            new = jnp.maximum(old, jnp.max(score, axis=1, keepdims=True) * SCALE2)
            weight = jnp.exp2(score * SCALE2 - new).astype(BF)
            acc[u] = acc[u] * jnp.exp2(old - new) + jnp.dot(
                weight, value_tile, preferred_element_type=F32
            )
            top[u] = new

    def start_chunk():
        top[...] = jnp.full_like(top, HIDDEN)
        acc[...] = jnp.zeros_like(acc)

    def project(c):
        for u in range(SUBS):
            mean = (acc[u, :, :HD] / acc[u, :, HD:]).astype(BF)
            for h in range(2):
                at = (2 * u + h) * HD
                att[:, at : at + HD] = mean[h * CHUNK : (h + 1) * CHUNK]

        def one(i, _):
            to_y = mod(y + 2 + div(i, 2), 4)
            to_z = mod(i, 2)
            columns = pl.ds(pl.multiple_of((to_y * 2 + to_z) * 1024, 1024), 1024)
            part = jnp.dot(att[...], w[:, columns], preferred_element_type=F32).astype(BF)
            pz[c, to_z * 4 + to_y] = part[:, :ZCOLS]
            py[c, to_z * 4 + to_y] = part[:, ZCOLS:]
            return 0

        lax.fori_loop(0, 8, one, 0)

    def to_y(src, dst, c, n, peer):
        return pltpu.make_async_remote_copy(
            src_ref=src, dst_ref=dst, send_sem=send.at[c, n], recv_sem=recv.at[c, n],
            device_id=(blk, peer), device_id_type=MESH,
        )

    y_up, y_down, y_far = mod(y + 1, 4), mod(y + 3, 4), mod(y + 2, 4)
    mine, other = zl * 4, (1 - zl) * 4
    lo, hi = pl.ds(0, 64), pl.ds(64, 64)

    def copy(c, n):
        if n == FAR:
            return to_y(py.at[c, y_far], far.at[c, 0], c, n, down)
        if n == FAR + 1:
            return to_y(py.at[c, 4 + y_far], far.at[c, 1], c, n, up)
        if n == NEAR:
            return to_y(py.at[c, y_down], near.at[c, 0], c, n, down)
        if n == NEAR + 1:
            return to_y(py.at[c, 4 + y_down], near.at[c, 1], c, n, down)
        if n == NEAR + 2:
            return to_y(py.at[c, y_up], near.at[c, 2], c, n, up)
        if n == NEAR + 3:
            return to_y(py.at[c, 4 + y_up], near.at[c, 3], c, n, up)
        if n == ZSUM:
            return to_y(py.at[c, other + y], zsum.at[c], c, n, zmate)
        if n == ZPRE:
            return to_y(pz.at[c, pl.ds(other, 4)], zpre.at[c], c, n, zmate)
        if n == ZFAR:
            return to_y(pz.at[c, mine + y_far, lo], zfar.at[c, 0], c, n, down)
        if n == ZFAR + 1:
            return to_y(pz.at[c, mine + y_far, hi], zfar.at[c, 1], c, n, up)
        if n == ZNEAR:
            return to_y(pz.at[c, mine + y_down, lo], znear.at[c, 0], c, n, down)
        if n == ZNEAR + 1:
            return to_y(pz.at[c, mine + y_down, hi], znear.at[c, 1], c, n, down)
        if n == ZNEAR + 2:
            return to_y(pz.at[c, mine + y_up, lo], znear.at[c, 2], c, n, up)
        return to_y(pz.at[c, mine + y_up, hi], znear.at[c, 3], c, n, up)

    def added(*parts):
        total = parts[0].astype(F32)
        for part in parts[1:]:
            total = total + part.astype(F32)
        return total.astype(BF)

    def stage_0(c):
        for n in (FAR, FAR + 1, ZPRE, NEAR + 1, NEAR + 2):
            copy(c, n).start()

    def stage_1(c):
        copy(c, FAR).wait_recv()
        py[c, y_down] = added(py[c, y_down], far[c, 0])
        copy(c, FAR + 1).wait_recv()
        py[c, 4 + y_up] = added(py[c, 4 + y_up], far[c, 1])
        copy(c, NEAR).start()
        copy(c, NEAR + 3).start()
        copy(c, ZPRE).wait_recv()
        for d in (2, 1, 3, 0):
            to = mod(y + d, 4)
            pz[c, mine + to] = added(pz[c, mine + to], zpre[c, to])
        for n in (ZFAR, ZFAR + 1, ZNEAR + 1, ZNEAR + 2):
            copy(c, n).start()

    def stage_2(c):
        copy(c, ZFAR).wait_recv()
        copy(c, ZFAR + 1).wait_recv()
        pz[c, mine + y_down, :64] = added(pz[c, mine + y_down, :64], zfar[c, 0])
        pz[c, mine + y_up, 64:] = added(pz[c, mine + y_up, 64:], zfar[c, 1])
        copy(c, ZNEAR).start()
        copy(c, ZNEAR + 3).start()
        for n in range(4):
            copy(c, NEAR + n).wait_recv()
        there = 1 - zl
        py[c, other + y] = added(py[c, other + y], near[c, there], near[c, 2 + there])
        copy(c, ZSUM).start()

    def stage_3(c):
        rows = pl.ds(pl.multiple_of(c * CHUNK, CHUNK), CHUNK)
        for n in range(4):
            copy(c, ZNEAR + n).wait_recv()
        first = pl.ds(pl.multiple_of(c * CHUNK, 64), 64)
        second = pl.ds(pl.multiple_of(c * CHUNK + 64, 64), 64)
        out[first, :ZCOLS] = added(pz[c, mine + y, :64], znear[c, 0], znear[c, 2])
        out[second, :ZCOLS] = added(pz[c, mine + y, 64:], znear[c, 1], znear[c, 3])
        copy(c, ZSUM).wait_recv()
        out[rows, ZCOLS:] = added(py[c, mine + y], near[c, zl], near[c, 2 + zl], zsum[c])

    def step(t, _):
        c = div(t, 4)
        s = mod(t, 4)
        for at, gather in enumerate((gather_0, gather_1, gather_2, gather_3)):
            pl.when(t == at)(gather)
        pl.when(s == 0)(start_chunk)
        attend(c, s)

        @pl.when((t >= 4) & (s == 0))
        def _():
            stage_1(c - 1)

        @pl.when((t >= 4) & (s == 2))
        def _():
            stage_2(c - 1)

        @pl.when((t >= 8) & (s == 0))
        def _():
            stage_3(c - 2)

        @pl.when(s == 3)
        def _():
            pl.when(t == 3)(w_copy.wait)
            project(c)
            stage_0(c)

        return 0

    lax.fori_loop(0, 4 * CHUNKS, step, 0)
    last = CHUNKS - 1
    stage_1(last)
    stage_3(last - 1)
    stage_2(last)
    stage_3(last)

    for n in range(len(kv_sends)):
        pltpu.make_async_remote_copy(
            src_ref=k, dst_ref=kv.at[blk, 0], send_sem=kv_send.at[n],
            recv_sem=kv_recv.at[blk, 0], device_id=(mate, head), device_id_type=MESH,
        ).wait_send()

    def sent(c, _):
        for n in range(14):
            copy(c, n).wait_send()
        return 0

    lax.fori_loop(0, CHUNKS, sent, 0)


def per_device(queries, keys, values, w_out, order):
    vmem = pl.BlockSpec(memory_space=pltpu.VMEM)
    return pl.pallas_call(
        kernel,
        out_shape=jax.ShapeDtypeStruct((CHUNK * CHUNKS, 1024), BF),
        in_specs=[pl.BlockSpec(memory_space=pltpu.SMEM), vmem, vmem, vmem,
                  pl.BlockSpec(memory_space=pl.ANY)],
        out_specs=vmem,
        scratch_shapes=[
            pltpu.VMEM((16, 2, 512, HD), BF),
            pltpu.VMEM((1024, 8192), BF),
            pltpu.VMEM((128, 128), BF),
            pltpu.VMEM((3, 128, 128), BF),
            pltpu.VMEM((SUBS, 256, 1), F32),
            pltpu.VMEM((SUBS, 256, 256), F32),
            pltpu.VMEM((CHUNK, 1024), BF),
            pltpu.VMEM((CHUNKS, 8, CHUNK, YCOLS), BF),
            pltpu.VMEM((CHUNKS, 8, CHUNK, ZCOLS), BF),
            pltpu.VMEM((CHUNKS, 2, CHUNK, YCOLS), BF),
            pltpu.VMEM((CHUNKS, 4, CHUNK, YCOLS), BF),
            pltpu.VMEM((CHUNKS, CHUNK, YCOLS), BF),
            pltpu.VMEM((CHUNKS, 4, CHUNK, ZCOLS), BF),
            pltpu.VMEM((CHUNKS, 2, 64, ZCOLS), BF),
            pltpu.VMEM((CHUNKS, 4, 64, ZCOLS), BF),
            pltpu.SemaphoreType.DMA((30,)),
            pltpu.SemaphoreType.DMA((16, 2)),
            pltpu.SemaphoreType.DMA((CHUNKS, 14)),
            pltpu.SemaphoreType.DMA((CHUNKS, 14)),
            pltpu.SemaphoreType.DMA,
        ],
        compiler_params=pltpu.CompilerParams(
            collective_id=0, has_side_effects=True, vmem_limit_bytes=66_000_000
        ),
        name="prefill",
    )(order, queries, keys, values, w_out)


def solution(mesh):
    placed = (P("blk", "head"), P("blk", "head"), P("blk", "head"), P("head", None), P())
    return jax.shard_map(
        per_device, mesh=mesh, in_specs=placed, out_specs=P("blk", "head"), check_vma=False
    )
```

time: 478 us -> 137 us (0.29)
  matrix products: 222 us -> 0 us
  waiting for transfers between devices: 173 us -> 0 us
  Pallas kernels: 0 us -> 134 us
  other arithmetic: 40.7 us -> 0 us
  local copies, waits for them, and re-layouts: 17.5 us -> 2.26 us
  between operations: 13.2 us -> 0.01 us
  loops' own time: 11.5 us -> 0 us
    dot_general x33 -> x0, matrix products: 222 us -> none  [the longest x16 130 us: attend(): jnp.einsum('kgtn,nkd->kgtd', weight.astype(jnp.bfloat16), v_block, prefer...]
    pallas_call x0 -> x1, Pallas kernels: none -> 134 us  [per_device(): pl.pallas_call(kernel, out_shape=jax.ShapeDtypeStruct((CHUNK * CHUNKS, 10...]
    reduce_scatter x2 -> x0, waiting for transfers between devices: 116 us -> none  [sum_by_axis(): value = lax.psum_scatter(value, axis, scatter_dimension=dim, tiled=True)]
    all_gather x1 -> x0, waiting for transfers between devices: 57.2 us -> none  [sent_together(): lax.all_gather(both, axis, axis=dim, tiled=True)]
    reduce_sum x33 -> x0, other arithmetic: 34.4 us -> none  [the longest x16 32.2 us: attend(): total = total * factor + jnp.sum(weight, axis=-1)]
    another operation x1 -> x0, loops' own time: 11.5 us -> none  [per_device(): lax.scan(one_block, start_state, (k_blocks, v_blocks, jnp.arange(steps, d...]
    dynamic_slice x16 -> x0, local copies, waits for them, and re-layouts: 9.38 us -> none  [per_device(): lax.scan(one_block, start_state, (k_blocks, v_blocks, jnp.arange(steps, d...]
  transfers between devices with their start and end apart: 3 -> 0, of which waited for: 3 -> 0; matrix products, arithmetic and copies ran while one was open for 1% -> 0% of each run, Pallas kernels for 0% -> 0%
where the time goes in v1:
time: 137 us; the launch traced here: 136 us
  Pallas kernels  134 us (98%)
  local copies, waits for them, and re-layouts  2.26 us (2%)
    pallas_call x1, Pallas kernels, per_device(): pl.pallas_call(kernel, out_shape=jax.ShapeDtypeStruct((CHUNK * CHUNKS, 10...  134 us

profile of v1, /device:TPU:0, one launch (start us, length us, event | category | flops | bytes accessed | tf_op | source)
XLA Modules:
  0.0 136.4 jit_solution(8358705662602951621)
XLA Ops:
  0.0 134.1 %prefill.1 = bf16[512,1024]{1,0:T(8,128)(2,1)} custom-call(s32[32]{0:T(128)} %order.1, bf16[512,1024]{1,0:T(8,128)(2,1)} %q.1, bf16[512,128]{1,0:T(8,128)(2,1)} %k.1, bf16[512,128]{1,0:T(8,128)(2,1)} %v.1, bf16[1024,8192]{1,0:T(8,128)(2,1)} %w_hbm.1), custom_call_target="tpu_custom_call" | custom-call | tf_op jit(solution)/shard_map/prefill/pallas_call | solution.py:349
  134.1 2.3 %copy.7 = bf16[512,1024]{1,0:T(8,128)(2,1)} copy(bf16[512,1024]{1,0:T(8,128)(2,1)} %prefill.1) | data formatting | bytes 2097152

commit v2 on v1

--- a/solution.py
+++ b/solution.py
@@ -98,63 +98,68 @@
     masks[1] = jnp.where(row > col, HIDDEN, 0.0).astype(BF)
     masks[2] = jnp.full((128, 128), HIDDEN, BF)
 
-    def gather_0():
+    def gather_a0():
         arrived(left, 0)
         pass_on(left, 0, right)
+        arrived(across, 0)
+        pass_on(across, 0, right)
+        pass_on(across, 0, left)
+
+    def gather_a2():
         arrived(right, 1)
         pass_on(right, 1, left)
+        arrived(across, 1)
+        pass_on(across, 1, right)
+        pass_on(across, 1, left)
         arrived(right, 0)
         arrived(left, 1)
+        for source in (right, left, across):
+            for part in (0, 1):
+                pass_on(source, part, mate)
+
+    def gather_1():
+        mate_has(0, 1)
+
+    def gather_2():
+        two, zleft = block(0, 2), block(1, 3)
         for part in (0, 1):
-            pass_on(right, part, mate)
-        for part in (0, 1):
-            pass_on(left, part, mate)
-        for part in (0, 1):
-            arrived(across, part)
-            pass_on(across, part, right)
-            pass_on(across, part, left)
-        for part in (0, 1):
-            pass_on(across, part, mate)
-        mate_has(0, 0)
-        mate_has(0, 1)
-
-    def gather_1():
-        far_block = block(0, 2)
-        for part in (0, 1):
-            arrived(far_block, part)
-            pass_on(far_block, part, mate)
-        mate_has(0, 3)
-        mate_has(1, 0)
-
-    def gather_2():
-        zleft, zright = block(1, 3), block(1, 1)
+            arrived(two, part)
+            pass_on(two, part, mate)
         arrived(zleft, 0)
         pass_on(zleft, 0, right)
+        mate_has(0, 3)
+
+    def gather_3():
+        mate_has(0, 2)
+
+    def gather_4():
+        zleft, zright = block(1, 3), block(1, 1)
         arrived(zright, 1)
         pass_on(zright, 1, left)
         arrived(zleft, 1)
         arrived(zright, 0)
-        for source in (zleft, zright):
+        for source in (zright, zleft):
             for part in (0, 1):
                 pass_on(source, part, mate)
-        mate_has(0, 2)
+        mate_has(1, 0)
+
+    def gather_5():
+        mate_has(1, 1)
+
+    def gather_6():
+        ztwo = block(1, 2)
+        for part in (0, 1):
+            arrived(ztwo, part)
+            pass_on(ztwo, part, mate)
         mate_has(1, 3)
 
-    def gather_3():
-        zfar_block = block(1, 2)
-        for part in (0, 1):
-            arrived(zfar_block, part)
-            pass_on(zfar_block, part, mate)
-        mate_has(1, 1)
+    def gather_7():
         mate_has(1, 2)
 
-    def attend(c, s):
+    def attend(c, places, first=False):
         rows = pl.ds(pl.multiple_of(c * CHUNK, CHUNK), CHUNK)
         query_pos = 2 * order[2 * blk + div(c, 2)] + mod(c, 2)
-        chips = (
-            mod(zh + div(s, 3), 2) * 4 + mod(x + 4 - s, 4),
-            mod(zh + div(s + 2, 3), 2) * 4 + mod(x + 5 - s, 4),
-        )
+        chips = [mod(zh + dz, 2) * 4 + mod(x + dx, 4) for dz, dx in places]
         key_rows, value_rows = [], []
         ones = jnp.ones((128, 128), BF)
         for chip in chips:
@@ -178,21 +183,18 @@
                 jnp.concatenate(q_rows, axis=0), key_tile,
                 (((1,), (1,)), ((), ())), preferred_element_type=F32,
             )
-            old = top[u]
-            new = jnp.maximum(old, jnp.max(score, axis=1, keepdims=True) * SCALE2)
+            new = jnp.max(score, axis=1, keepdims=True) * SCALE2
+            if not first:
+                old = top[c, u]
+                new = jnp.maximum(old, new)
             weight = jnp.exp2(score * SCALE2 - new).astype(BF)
-            acc[u] = acc[u] * jnp.exp2(old - new) + jnp.dot(
-                weight, value_tile, preferred_element_type=F32
-            )
-            top[u] = new
-
-    def start_chunk():
-        top[...] = jnp.full_like(top, HIDDEN)
-        acc[...] = jnp.zeros_like(acc)
+            part = jnp.dot(weight, value_tile, preferred_element_type=F32)
+            acc[c, u] = part if first else acc[c, u] * jnp.exp2(old - new) + part
+            top[c, u] = new
 
     def project(c):
         for u in range(SUBS):
-            mean = (acc[u, :, :HD] / acc[u, :, HD:]).astype(BF)
+            mean = (acc[c, u, :, :HD] / acc[c, u, :, HD:]).astype(BF)
             for h in range(2):
                 at = (2 * u + h) * HD
                 att[:, at : at + HD] = mean[h * CHUNK : (h + 1) * CHUNK]
@@ -264,6 +266,8 @@
         py[c, 4 + y_up] = added(py[c, 4 + y_up], far[c, 1])
         copy(c, NEAR).start()
         copy(c, NEAR + 3).start()
+
+    def stage_1b(c):
         copy(c, ZPRE).wait_recv()
         for d in (2, 1, 3, 0):
             to = mod(y + d, 4)
@@ -272,17 +276,17 @@
             copy(c, n).start()
 
     def stage_2(c):
+        for n in range(4):
+            copy(c, NEAR + n).wait_recv()
+        there = 1 - zl
+        py[c, other + y] = added(py[c, other + y], near[c, there], near[c, 2 + there])
+        copy(c, ZSUM).start()
         copy(c, ZFAR).wait_recv()
         copy(c, ZFAR + 1).wait_recv()
         pz[c, mine + y_down, :64] = added(pz[c, mine + y_down, :64], zfar[c, 0])
         pz[c, mine + y_up, 64:] = added(pz[c, mine + y_up, 64:], zfar[c, 1])
         copy(c, ZNEAR).start()
         copy(c, ZNEAR + 3).start()
-        for n in range(4):
-            copy(c, NEAR + n).wait_recv()
-        there = 1 - zl
-        py[c, other + y] = added(py[c, other + y], near[c, there], near[c, 2 + there])
-        copy(c, ZSUM).start()
 
     def stage_3(c):
         rows = pl.ds(pl.multiple_of(c * CHUNK, CHUNK), CHUNK)
@@ -295,38 +299,52 @@
         copy(c, ZSUM).wait_recv()
         out[rows, ZCOLS:] = added(py[c, mine + y], near[c, zl], near[c, 2 + zl], zsum[c])
 
-    def step(t, _):
-        c = div(t, 4)
-        s = mod(t, 4)
-        for at, gather in enumerate((gather_0, gather_1, gather_2, gather_3)):
-            pl.when(t == at)(gather)
-        pl.when(s == 0)(start_chunk)
-        attend(c, s)
-
-        @pl.when((t >= 4) & (s == 0))
+    def early(c, _):
+        attend(c, ((0, 0),), first=True)
+        pl.when(c == 1)(gather_a0)
+        pl.when(c == 2)(gather_a2)
+        return 0
+
+    waits = (gather_1, gather_2, gather_3, gather_4, gather_5, gather_6, gather_7)
+
+    def one_chip(n, _):
+        for at, gather in enumerate(waits):
+            pl.when(n == at + 1)(gather)
+        m = mod(n, 4)
+        attend(0, ((div(n, 4), m + div(m, 2) - 2 * div(m, 3)),))
+        return 0
+
+    def step(n, _):
+        c = div(n, 3)
+        s = mod(n, 3)
+        attend(c, ((div(s + 1, 2), mod(s + 1, 2)), (div(s, 2), 3 - mod(s, 2))))
+
+        @pl.when(s == 1)
         def _():
             stage_1(c - 1)
-
-        @pl.when((t >= 4) & (s == 2))
+            pl.when(c >= 2)(lambda: stage_3(c - 2))
+
+        @pl.when(s == 2)
         def _():
+            stage_1b(c - 1)
+            attend(c, ((1, 2),))
+            project(c)
             stage_2(c - 1)
-
-        @pl.when((t >= 8) & (s == 0))
-        def _():
-            stage_3(c - 2)
-
-        @pl.when(s == 3)
-        def _():
-            pl.when(t == 3)(w_copy.wait)
-            project(c)
             stage_0(c)
 
         return 0
 
-    lax.fori_loop(0, 4 * CHUNKS, step, 0)
+    mate_has(0, 0)
+    lax.fori_loop(0, CHUNKS, early, 0)
+    lax.fori_loop(1, 8, one_chip, 0)
+    w_copy.wait()
+    project(0)
+    stage_0(0)
+    lax.fori_loop(3, 3 * CHUNKS, step, 0)
     last = CHUNKS - 1
     stage_1(last)
     stage_3(last - 1)
+    stage_1b(last)
     stage_2(last)
     stage_3(last)
 
@@ -357,8 +375,8 @@
             pltpu.VMEM((1024, 8192), BF),
             pltpu.VMEM((128, 128), BF),
             pltpu.VMEM((3, 128, 128), BF),
-            pltpu.VMEM((SUBS, 256, 1), F32),
-            pltpu.VMEM((SUBS, 256, 256), F32),
+            pltpu.VMEM((CHUNKS, SUBS, 256, 1), F32),
+            pltpu.VMEM((CHUNKS, SUBS, 256, 256), F32),
             pltpu.VMEM((CHUNK, 1024), BF),
             pltpu.VMEM((CHUNKS, 8, CHUNK, YCOLS), BF),
             pltpu.VMEM((CHUNKS, 8, CHUNK, ZCOLS), BF),

time: 137 us -> 116 us (0.85)
  Pallas kernels: 134 us -> 114 us
    pallas_call x1, Pallas kernels: 134 us -> 114 us  [per_device(): pl.pallas_call(kernel, out_shape=jax.ShapeDtypeStruct((CHUNK * CHUNKS, 10...]
where the time goes in v2:
time: 116 us
  Pallas kernels  114 us (98%)
  local copies, waits for them, and re-layouts  2.26 us (2%)
    pallas_call x1, Pallas kernels, per_device(): pl.pallas_call(kernel, out_shape=jax.ShapeDtypeStruct((CHUNK * CHUNKS, 10...  114 us

profile of v2, /device:TPU:0, one launch (start us, length us, event | category | flops | bytes accessed | tf_op | source)
XLA Modules:
  0.0 115.8 jit_solution(7160627247623262061)
XLA Ops:
  0.0 113.5 %prefill.1 = bf16[512,1024]{1,0:T(8,128)(2,1)} custom-call(s32[32]{0:T(128)} %order.1, bf16[512,1024]{1,0:T(8,128)(2,1)} %q.1, bf16[512,128]{1,0:T(8,128)(2,1)} %k.1, bf16[512,128]{1,0:T(8,128)(2,1)} %v.1, bf16[1024,8192]{1,0:T(8,128)(2,1)} %w_hbm.1), custom_call_target="tpu_custom_call" | custom-call | tf_op jit(solution)/shard_map/prefill/pallas_call | solution.py:367
  113.5 2.3 %copy.7 = bf16[512,1024]{1,0:T(8,128)(2,1)} copy(bf16[512,1024]{1,0:T(8,128)(2,1)} %prefill.1) | data formatting | bytes 2097152

commit v3 on v2

--- a/solution.py
+++ b/solution.py
@@ -29,10 +29,10 @@
 
 
 def kernel(
-    order, q, k, v, w_hbm, out,
-    kv, w, eye, masks, top, acc, att,
+    order, q_hbm, k, v, w_hbm, out,
+    q, kv, w, eye, masks, top, acc, att,
     py, pz, far, near, zsum, zpre, zfar, znear,
-    kv_send, kv_recv, send, recv, w_sem,
+    kv_send, kv_recv, send, recv, w_sem, in_sem,
 ):
     blk = lax.axis_index("blk")
     head = lax.axis_index("head")
@@ -51,6 +51,12 @@
     down = mod(y + 3, 4) * 2 + zl
     zmate = head + 1 - 2 * zl
 
+    loads = [
+        pltpu.make_async_copy(src, dst, in_sem.at[n])
+        for n, (src, dst) in enumerate(((q_hbm, q), (k, kv.at[blk, 0]), (v, kv.at[blk, 1])))
+    ]
+    for load in loads:
+        load.start()
     barrier = pltpu.get_barrier_semaphore()
     for peer in (left, right, across, mate):
         pl.semaphore_signal(barrier, inc=1, device_id=(peer, head), device_id_type=MESH)
@@ -89,8 +95,6 @@
             pass_on(blk, part, to, own=True)
     w_copy.start()
 
-    kv[blk, 0] = k[...]
-    kv[blk, 1] = v[...]
     row = lax.broadcasted_iota(jnp.int32, (128, 128), 0)
     col = lax.broadcasted_iota(jnp.int32, (128, 128), 1)
     eye[...] = jnp.where(row == col, 1.0, 0.0).astype(BF)
@@ -200,15 +204,15 @@
                 att[:, at : at + HD] = mean[h * CHUNK : (h + 1) * CHUNK]
 
         def one(i, _):
-            to_y = mod(y + 2 + div(i, 2), 4)
-            to_z = mod(i, 2)
-            columns = pl.ds(pl.multiple_of((to_y * 2 + to_z) * 1024, 1024), 1024)
+            to = mod(y + 2 + i, 4)
+            columns = pl.ds(pl.multiple_of(to * 2048, 2048), 2048)
             part = jnp.dot(att[...], w[:, columns], preferred_element_type=F32).astype(BF)
-            pz[c, to_z * 4 + to_y] = part[:, :ZCOLS]
-            py[c, to_z * 4 + to_y] = part[:, ZCOLS:]
+            for z in range(2):
+                pz[c, z * 4 + to] = part[:, z * 1024 : z * 1024 + ZCOLS]
+                py[c, z * 4 + to] = part[:, z * 1024 + ZCOLS : (z + 1) * 1024]
             return 0
 
-        lax.fori_loop(0, 8, one, 0)
+        lax.fori_loop(0, 4, one, 0)
 
     def to_y(src, dst, c, n, peer):
         return pltpu.make_async_remote_copy(
@@ -256,7 +260,7 @@
         return total.astype(BF)
 
     def stage_0(c):
-        for n in (FAR, FAR + 1, ZPRE, NEAR + 1, NEAR + 2):
+        for n in (ZPRE, FAR, FAR + 1, NEAR + 1, NEAR + 2):
             copy(c, n).start()
 
     def stage_1(c):
@@ -322,18 +326,20 @@
         @pl.when(s == 1)
         def _():
             stage_1(c - 1)
-            pl.when(c >= 2)(lambda: stage_3(c - 2))
 
         @pl.when(s == 2)
         def _():
+            attend(c, ((1, 2),))
             stage_1b(c - 1)
-            attend(c, ((1, 2),))
             project(c)
+            stage_0(c)
             stage_2(c - 1)
-            stage_0(c)
+            pl.when(c >= 2)(lambda: stage_3(c - 2))
 
         return 0
 
+    for load in loads:
+        load.wait()
     mate_has(0, 0)
     lax.fori_loop(0, CHUNKS, early, 0)
     lax.fori_loop(1, 8, one_chip, 0)
@@ -367,10 +373,10 @@
     return pl.pallas_call(
         kernel,
         out_shape=jax.ShapeDtypeStruct((CHUNK * CHUNKS, 1024), BF),
-        in_specs=[pl.BlockSpec(memory_space=pltpu.SMEM), vmem, vmem, vmem,
-                  pl.BlockSpec(memory_space=pl.ANY)],
+        in_specs=[pl.BlockSpec(memory_space=pltpu.SMEM)] + [pl.BlockSpec(memory_space=pl.ANY)] * 4,
         out_specs=vmem,
         scratch_shapes=[
+            pltpu.VMEM((CHUNK * CHUNKS, 1024), BF),
             pltpu.VMEM((16, 2, 512, HD), BF),
             pltpu.VMEM((1024, 8192), BF),
             pltpu.VMEM((128, 128), BF),
@@ -391,6 +397,7 @@
             pltpu.SemaphoreType.DMA((CHUNKS, 14)),
             pltpu.SemaphoreType.DMA((CHUNKS, 14)),
             pltpu.SemaphoreType.DMA,
+            pltpu.SemaphoreType.DMA((3,)),
         ],
         compiler_params=pltpu.CompilerParams(
             collective_id=0, has_side_effects=True, vmem_limit_bytes=66_000_000

time: 116 us -> 109 us (0.940)
  Pallas kernels: 114 us -> 107 us
    pallas_call x1, Pallas kernels: 114 us -> 107 us  [per_device(): pl.pallas_call(kernel, out_shape=jax.ShapeDtypeStruct((CHUNK * CHUNKS, 10...]
where the time goes in v3:
time: 109 us
  Pallas kernels  107 us (98%)
  local copies, waits for them, and re-layouts  2.26 us (2%)
    pallas_call x1, Pallas kernels, per_device(): pl.pallas_call(kernel, out_shape=jax.ShapeDtypeStruct((CHUNK * CHUNKS, 10...  107 us
    unnamed x1, local copies, waits for them, and re-layouts  2.26 us

profile of v3, /device:TPU:0, one launch (start us, length us, event | category | flops | bytes accessed | tf_op | source)
XLA Modules:
  0.0 109.1 jit_solution(15308926766857743340)
XLA Ops:
  0.0 106.8 %prefill.1 = bf16[512,1024]{1,0:T(8,128)(2,1)} custom-call(s32[32]{0:T(128)} %order.1, bf16[512,1024]{1,0:T(8,128)(2,1)} %q_hbm.1, bf16[512,128]{1,0:T(8,128)(2,1)} %k.1, bf16[512,128]{1,0:T(8,128)(2,1)} %v.1, bf16[1024,8192]{1,0:T(8,128)(2,1)} %w_hbm.1), custom_call_target="tpu_custom_call" | custom-call | tf_op jit(solution)/shard_map/prefill/pallas_call | solution.py:373
  106.8 2.3 %copy.7 = bf16[512,1024]{1,0:T(8,128)(2,1)} copy(bf16[512,1024]{1,0:T(8,128)(2,1)} %prefill.1) | data formatting | bytes 2097152

commit v4 on v3

--- a/solution.py
+++ b/solution.py
@@ -178,23 +178,29 @@
                     value_rows.append(jnp.concatenate([kv[b, 1, part, :], ones], axis=1))
         key_tile = jnp.concatenate(key_rows, axis=0)
         value_tile = jnp.concatenate(value_rows, axis=0)
+        scores = []
         for u in range(SUBS):
             q_rows = [
                 jnp.concatenate([q[rows, h * HD : (h + 1) * HD], eye[...]], axis=1)
                 for h in (2 * u, 2 * u + 1)
             ]
-            score = lax.dot_general(
+            scores.append(lax.dot_general(
                 jnp.concatenate(q_rows, axis=0), key_tile,
                 (((1,), (1,)), ((), ())), preferred_element_type=F32,
-            )
+            ))
+        weights = []
+        for u, score in enumerate(scores):
             new = jnp.max(score, axis=1, keepdims=True) * SCALE2
+            fade = None
             if not first:
                 old = top[c, u]
                 new = jnp.maximum(old, new)
-            weight = jnp.exp2(score * SCALE2 - new).astype(BF)
+                fade = jnp.exp2(old - new)
+            top[c, u] = new
+            weights.append((jnp.exp2(score * SCALE2 - new).astype(BF), fade))
+        for u, (weight, fade) in enumerate(weights):
             part = jnp.dot(weight, value_tile, preferred_element_type=F32)
-            acc[c, u] = part if first else acc[c, u] * jnp.exp2(old - new) + part
-            top[c, u] = new
+            acc[c, u] = part if first else acc[c, u] * fade + part
 
     def project(c):
         for u in range(SUBS):

time: 109 us -> 102 us (0.936)
  Pallas kernels: 107 us -> 98.9 us
    pallas_call x1, Pallas kernels: 107 us -> 98.9 us  [per_device(): pl.pallas_call(kernel, out_shape=jax.ShapeDtypeStruct((CHUNK * CHUNKS, 10...]
where the time goes in v4:
time: 102 us; the launch traced here: 101 us
  Pallas kernels  98.9 us (97%)
  local copies, waits for them, and re-layouts  2.26 us (2%)
    pallas_call x1, Pallas kernels, per_device(): pl.pallas_call(kernel, out_shape=jax.ShapeDtypeStruct((CHUNK * CHUNKS, 10...  98.9 us
    unnamed x1, local copies, waits for them, and re-layouts  2.26 us

profile of v4, /device:TPU:0, one launch (start us, length us, event | category | flops | bytes accessed | tf_op | source)
XLA Modules:
  0.0 101.2 jit_solution(16008033886707482052)
XLA Ops:
  0.0 98.9 %prefill.1 = bf16[512,1024]{1,0:T(8,128)(2,1)} custom-call(s32[32]{0:T(128)} %order.1, bf16[512,1024]{1,0:T(8,128)(2,1)} %q_hbm.1, bf16[512,128]{1,0:T(8,128)(2,1)} %k.1, bf16[512,128]{1,0:T(8,128)(2,1)} %v.1, bf16[1024,8192]{1,0:T(8,128)(2,1)} %w_hbm.1), custom_call_target="tpu_custom_call" | custom-call | tf_op jit(solution)/shard_map/prefill/pallas_call | solution.py:379
  99.0 2.3 %copy.7 = bf16[512,1024]{1,0:T(8,128)(2,1)} copy(bf16[512,1024]{1,0:T(8,128)(2,1)} %prefill.1) | data formatting | bytes 2097152

commit v5 on v4

--- a/solution.py
+++ b/solution.py
@@ -216,6 +216,16 @@
             for z in range(2):
                 pz[c, z * 4 + to] = part[:, z * 1024 : z * 1024 + ZCOLS]
                 py[c, z * 4 + to] = part[:, z * 1024 + ZCOLS : (z + 1) * 1024]
+
+            @pl.when(i == 1)
+            def _():
+                copy(c, FAR).start()
+                copy(c, FAR + 1).start()
+
+            @pl.when(i == 2)
+            def _():
+                copy(c, NEAR + 1).start()
+
             return 0
 
         lax.fori_loop(0, 4, one, 0)
@@ -266,7 +276,7 @@
         return total.astype(BF)
 
     def stage_0(c):
-        for n in (ZPRE, FAR, FAR + 1, NEAR + 1, NEAR + 2):
+        for n in (ZPRE, NEAR + 2):
             copy(c, n).start()
 
     def stage_1(c):
@@ -291,6 +301,8 @@
         there = 1 - zl
         py[c, other + y] = added(py[c, other + y], near[c, there], near[c, 2 + there])
         copy(c, ZSUM).start()
+
+    def stage_2z(c):
         copy(c, ZFAR).wait_recv()
         copy(c, ZFAR + 1).wait_recv()
         pz[c, mine + y_down, :64] = added(pz[c, mine + y_down, :64], zfar[c, 0])
@@ -329,6 +341,10 @@
         s = mod(n, 3)
         attend(c, ((div(s + 1, 2), mod(s + 1, 2)), (div(s, 2), 3 - mod(s, 2))))
 
+        @pl.when((s == 0) & (c >= 2))
+        def _():
+            stage_2z(c - 2)
+
         @pl.when(s == 1)
         def _():
             stage_1(c - 1)
@@ -354,10 +370,12 @@
     stage_0(0)
     lax.fori_loop(3, 3 * CHUNKS, step, 0)
     last = CHUNKS - 1
+    stage_2z(last - 1)
     stage_1(last)
-    stage_3(last - 1)
     stage_1b(last)
     stage_2(last)
+    stage_3(last - 1)
+    stage_2z(last)
     stage_3(last)
 
     for n in range(len(kv_sends)):

time: 102 us -> 99.4 us (0.975)
  Pallas kernels: 98.9 us -> 97 us
    pallas_call x1, Pallas kernels: 98.9 us -> 97 us  [per_device(): pl.pallas_call(kernel, out_shape=jax.ShapeDtypeStruct((CHUNK * CHUNKS, 10...]
where the time goes in v5:
time: 99.4 us; the launch traced here: 99.3 us
  Pallas kernels  97 us (98%)
  local copies, waits for them, and re-layouts  2.26 us (2%)
    pallas_call x1, Pallas kernels, per_device(): pl.pallas_call(kernel, out_shape=jax.ShapeDtypeStruct((CHUNK * CHUNKS, 10...  97 us
    unnamed x1, local copies, waits for them, and re-layouts  2.26 us

profile of v5, /device:TPU:0, one launch (start us, length us, event | category | flops | bytes accessed | tf_op | source)
XLA Modules:
  0.0 99.3 jit_solution(7368177943026013957)
XLA Ops:
  0.0 97.0 %prefill.1 = bf16[512,1024]{1,0:T(8,128)(2,1)} custom-call(s32[32]{0:T(128)} %order.1, bf16[512,1024]{1,0:T(8,128)(2,1)} %q_hbm.1, bf16[512,128]{1,0:T(8,128)(2,1)} %k.1, bf16[512,128]{1,0:T(8,128)(2,1)} %v.1, bf16[1024,8192]{1,0:T(8,128)(2,1)} %w_hbm.1), custom_call_target="tpu_custom_call" | custom-call | tf_op jit(solution)/shard_map/prefill/pallas_call | solution.py:397
  97.0 2.3 %copy.7 = bf16[512,1024]{1,0:T(8,128)(2,1)} copy(bf16[512,1024]{1,0:T(8,128)(2,1)} %prefill.1) | data formatting | bytes 2097152

commit v6 on v5

--- a/solution.py
+++ b/solution.py
@@ -226,6 +226,10 @@
             def _():
                 copy(c, NEAR + 1).start()
 
+            @pl.when(i >= 1)
+            def _():
+                across_z(c, i - 1).start()
+
             return 0
 
         lax.fori_loop(0, 4, one, 0)
@@ -255,8 +259,6 @@
             return to_y(py.at[c, 4 + y_up], near.at[c, 3], c, n, up)
         if n == ZSUM:
             return to_y(py.at[c, other + y], zsum.at[c], c, n, zmate)
-        if n == ZPRE:
-            return to_y(pz.at[c, pl.ds(other, 4)], zpre.at[c], c, n, zmate)
         if n == ZFAR:
             return to_y(pz.at[c, mine + y_far, lo], zfar.at[c, 0], c, n, down)
         if n == ZFAR + 1:
@@ -269,6 +271,10 @@
             return to_y(pz.at[c, mine + y_up, lo], znear.at[c, 2], c, n, up)
         return to_y(pz.at[c, mine + y_up, hi], znear.at[c, 3], c, n, up)
 
+    def across_z(c, d):
+        to = mod(y + 2 + d, 4)
+        return to_y(pz.at[c, other + to], zpre.at[c, to], c, 14 + d, zmate)
+
     def added(*parts):
         total = parts[0].astype(F32)
         for part in parts[1:]:
@@ -276,8 +282,8 @@
         return total.astype(BF)
 
     def stage_0(c):
-        for n in (ZPRE, NEAR + 2):
-            copy(c, n).start()
+        across_z(c, 3).start()
+        copy(c, NEAR + 2).start()
 
     def stage_1(c):
         copy(c, FAR).wait_recv()
@@ -288,12 +294,12 @@
         copy(c, NEAR + 3).start()
 
     def stage_1b(c):
-        copy(c, ZPRE).wait_recv()
-        for d in (2, 1, 3, 0):
-            to = mod(y + d, 4)
+        for d, sends in enumerate(((ZFAR, ZFAR + 1), (ZNEAR + 1,), (), (ZNEAR + 2,))):
+            across_z(c, d).wait_recv()
+            to = mod(y + 2 + d, 4)
             pz[c, mine + to] = added(pz[c, mine + to], zpre[c, to])
-        for n in (ZFAR, ZFAR + 1, ZNEAR + 1, ZNEAR + 2):
-            copy(c, n).start()
+            for n in sends:
+                copy(c, n).start()
 
     def stage_2(c):
         for n in range(4):
@@ -386,7 +392,10 @@
 
     def sent(c, _):
         for n in range(14):
-            copy(c, n).wait_send()
+            if n != ZPRE:
+                copy(c, n).wait_send()
+        for d in range(4):
+            across_z(c, d).wait_send()
         return 0
 
     lax.fori_loop(0, CHUNKS, sent, 0)
@@ -418,8 +427,8 @@
             pltpu.VMEM((CHUNKS, 4, 64, ZCOLS), BF),
             pltpu.SemaphoreType.DMA((30,)),
             pltpu.SemaphoreType.DMA((16, 2)),
-            pltpu.SemaphoreType.DMA((CHUNKS, 14)),
-            pltpu.SemaphoreType.DMA((CHUNKS, 14)),
+            pltpu.SemaphoreType.DMA((CHUNKS, 18)),
+            pltpu.SemaphoreType.DMA((CHUNKS, 18)),
             pltpu.SemaphoreType.DMA,
             pltpu.SemaphoreType.DMA((3,)),
         ],

time: 99.4 us -> 98.9 us (level)
  no operation moved by 1% of the time
where the time goes in v6:
time: 98.9 us; the launch traced here: 98.7 us
  Pallas kernels  96.5 us (98%)
  local copies, waits for them, and re-layouts  2.26 us (2%)
    pallas_call x1, Pallas kernels, per_device(): pl.pallas_call(kernel, out_shape=jax.ShapeDtypeStruct((CHUNK * CHUNKS, 10...  96.5 us
    unnamed x1, local copies, waits for them, and re-layouts  2.26 us

profile of v6, /device:TPU:0, one launch (start us, length us, event | category | flops | bytes accessed | tf_op | source)
XLA Modules:
  0.0 98.7 jit_solution(7873310387392183510)
XLA Ops:
  0.0 96.5 %prefill.1 = bf16[512,1024]{1,0:T(8,128)(2,1)} custom-call(s32[32]{0:T(128)} %order.1, bf16[512,1024]{1,0:T(8,128)(2,1)} %q_hbm.1, bf16[512,128]{1,0:T(8,128)(2,1)} %k.1, bf16[512,128]{1,0:T(8,128)(2,1)} %v.1, bf16[1024,8192]{1,0:T(8,128)(2,1)} %w_hbm.1), custom_call_target="tpu_custom_call" | custom-call | tf_op jit(solution)/shard_map/prefill/pallas_call | solution.py:406
  96.5 2.3 %copy.7 = bf16[512,1024]{1,0:T(8,128)(2,1)} copy(bf16[512,1024]{1,0:T(8,128)(2,1)} %prefill.1) | data formatting | bytes 2097152
